TPU v7x, 512 devices: a whole 4x8x8 slice. The times are simulated.
512 devices in a mesh: dp: 16 (over y, core), table: 32 (over x, z).
Axes of the slice: x: 4, y: 8, z: 8, core: 2. Of those that a mesh axis runs over, the one named last changes fastest.
Arguments:
- embedded: bfloat16 [2, 32768, 4096], P(None, 'dp', 'table'), may hold values from -1.1953125 to 1.1953125
- resid_grad: bfloat16 [2, 32768, 4096], P(None, 'dp', 'table'), may hold values from -0.29882812 to 0.29882812
- query_grad: bfloat16 [2, 32768, 2048], P(None, ('dp', 'table')), may hold values from -0.59765625 to 0.59765625
- query_weight: bfloat16 [4096, 2048], P('table'), may hold values from -0.09375 to 0.09375
- ngram_rows: int32 [2, 32768, 4], P(None, 'dp'), may hold values from 0 to 3199999, as said below
- touched_rows: int32 [32, 4, 12], replicated, may hold values from -1 to 3199999, as said below
- row_values: float32 [32, 4, 12, 1024], P('table'), may hold values from -6 to 6
- row_mean: float32 [32, 4, 12, 1024], P('table'), may hold values from -0.6 to 0.6
- row_square: float32 [32, 4, 12, 1024], P('table'), may hold values from 0.01 to 0.1
Outputs:
- weight_grad: float32 [4096, 2048], P('table')
- new_values: float32 [32, 4, 12, 1024], P('table')
- new_mean: float32 [32, 4, 12, 1024], P('table')
- new_square: float32 [32, 4, 12, 1024], P('table')
Inputs may be any that keep to these rules, and one draw needn't show every extreme that they name: `touched_rows`: owner o's list for slice s holds 1 to 12 distinct row ids of [o * 100000, (o + 1) * 100000) first, then -1; in every slice some owner's list is full. `ngram_rows`: every id of slice s is one of the listed rows of owner id // 100000 for slice s.
All inputs are finite; a program needn't handle non-finite values.
Results may differ from a plain program's by a relative error of at most 0.0003.
Values may be sent and summed in bfloat16 or wider, within the bound.
No kernel may reach another device: no remote copies, remote signals or barrier semaphores. Data moves between devices by JAX's collectives and lax.ppermute only.
A program may use at most 64 MiB of HBM per device.

v0:
```python
import jax
import jax.numpy as jnp
from jax import lax
from jax.sharding import PartitionSpec as P

SLICES = 4
SW = 1024
beta_one = 0.9
beta_two = 0.95
learn_rate = 0.01
adam_eps = 1e-08
adam_step = 10


def adam_rows(grads, values, mean, square, live):
    corr_one = 1.0 - beta_one**adam_step
    corr_two = 1.0 - beta_two**adam_step
    mean_next = beta_one * mean + (1.0 - beta_one) * grads
    square_next = beta_two * square + (1.0 - beta_two) * grads * grads
    update = learn_rate * (mean_next / corr_one) / (jnp.sqrt(square_next / corr_two) + adam_eps)
    values_next = values - update
    return (
        jnp.where(live, values_next, values),
        jnp.where(live, mean_next, mean),
        jnp.where(live, square_next, square),
    )


def make_step(emb_part, weight_part, carry, piece):
    back_part, wgrad = carry
    back = jnp.einsum("mrh,ph->mrp", piece, weight_part, preferred_element_type=jnp.float32)
    back_part = back
    wgrad = wgrad + jnp.einsum("mrp,mrh->ph", emb_part, piece, preferred_element_type=jnp.float32)
    return (back_part, wgrad)


def local(
    embedded,
    resid_grad,
    query_grad,
    query_weight,
    ngram_rows,
    touched_rows,
    row_values,
    row_mean,
    row_square,
):
    micro_count, group_tokens, width_part = embedded.shape
    hidden = query_grad.shape[2]
    tables = lax.axis_size("table")
    table_idx = lax.axis_index("table")
    zero_grad = jnp.zeros((width_part, hidden), jnp.float32)
    wgrad = zero_grad
    backs = []
    for micro in range(micro_count):
        start_back = jnp.zeros((1, group_tokens, width_part), jnp.float32)
        back_one, wgrad = make_step(
            embedded[micro : micro + 1],
            query_weight,
            (start_back, wgrad),
            lax.all_gather(query_grad[micro : micro + 1], "table", axis=1, tiled=True),
        )
        backs.append(back_one)
    back_all = jnp.concatenate(backs, axis=0)
    emb_grad = resid_grad.astype(jnp.float32) + back_all
    weight_grad = lax.psum(wgrad, "dp")
    slice_idx = table_idx * width_part // SW
    ids = lax.dynamic_index_in_dim(ngram_rows, slice_idx, 2, False)
    listed = lax.dynamic_index_in_dim(touched_rows, slice_idx, 1, False)
    entries = listed.shape[1]
    flat_list = listed.reshape(tables * entries)
    onehot = (ids[:, :, None] == flat_list[None, None, :]).astype(jnp.float32)
    buckets = jnp.einsum(
        "mtk,mtp->kp",
        onehot,
        emb_grad,
        precision=lax.Precision.HIGHEST,
        preferred_element_type=jnp.float32,
    )
    buckets = buckets.reshape(tables, entries, width_part)
    arrived = lax.all_to_all(buckets, "table", split_axis=0, concat_axis=0, tiled=True)
    per_slice = tables // SLICES
    local_grad = (
        arrived.reshape(SLICES, per_slice, entries, width_part)
        .transpose(0, 2, 1, 3)
        .reshape(SLICES, entries, per_slice * width_part)
    )
    mine = lax.dynamic_index_in_dim(touched_rows, table_idx, 0, False)
    live = (mine >= 0)[..., None]
    values = row_values[0]
    mean = row_mean[0]
    square = row_square[0]
    grads = lax.psum(local_grad, "dp")
    values_next, mean_next, square_next = adam_rows(grads, values, mean, square, live)
    return (weight_grad, values_next[None], mean_next[None], square_next[None])


def solution(mesh):
    placed = (
        P(None, "dp", "table"),
        P(None, "dp", "table"),
        P(None, ("dp", "table"), None),
        P("table", None),
        P(None, "dp", None),
        P(),
        P("table", None, None, None),
        P("table", None, None, None),
        P("table", None, None, None),
    )
    return jax.shard_map(
        local,
        mesh=mesh,
        in_specs=placed,
        out_specs=(
            P("table", None),
            P("table", None, None, None),
            P("table", None, None, None),
            P("table", None, None, None),
        ),
        check_vma=False,
    )
```

profile of v0, /device:TPU:25, one launch (start us, length us, event | category | flops | bytes accessed | tf_op | source)
XLA Modules:
  0.0 381.5 jit_solution(2230396503521548309)
XLA Ops:
  7.2 1.9 fusion.37
  9.2 0.7 all-gather.3.cloned.1.call-update
  9.9 0.9 constant_dynamic-slice_fusion.1
  10.8 0.8 constant_dynamic-slice_fusion
  11.6 0.1 copy.22
  11.7 0.1 eq.19
  11.8 107.7 %all-gather.5.cloned.1.call-done = bf16[1,2048,2048]{2,1,0:T(8,128)(2,1)} async-done(((bf16[1,64,2048]{2,1,0:T(8,128)(2,1)}), bf16[1,2048,2048]{2,1,0:T(8,128)(2,1)}) %all-gather.5.cloned.1.call-update) | async-done | bytes 8388624 | tf_op jit(solution)/shard_map/all_gather | solution.py:61
  119.5 6.7 %fusion.15 = f32[1,2048,128]{2,1,0:T(8,128)} fusion(bf16[128,2048]{1,0:T(8,128)(2,1)S(1)} %copy-done, bf16[1,2048,2048]{2,1,0:T(8,128)(2,1)} %all-gather.5.cloned.1.call-done), kind=kOutput, calls=%fused_computation.13 | convolution fusion | flops 1073741824 | bytes 9961472 | tf_op jit(solution)/shard_map/mrh,ph->mrp/dot_general | solution.py:31
  126.2 97.1 %all-gather.3.cloned.1.call-done = bf16[1,2048,2048]{2,1,0:T(8,128)(2,1)} async-done(((bf16[1,64,2048]{2,1,0:T(8,128)(2,1)}), bf16[1,2048,2048]{2,1,0:T(8,128)(2,1)}) %all-gather.3.cloned.1.call-update) | async-done | bytes 8388624 | tf_op jit(solution)/shard_map/all_gather | solution.py:61
  223.3 5.9 %fusion.12 = f32[1,2048,128]{2,1,0:T(8,128)S(1)} fusion(bf16[128,2048]{1,0:T(8,128)(2,1)S(1)} %copy-done, bf16[1,2048,2048]{2,1,0:T(8,128)(2,1)} %all-gather.3.cloned.1.call-done), kind=kOutput, calls=%fused_computation.12 | convolution fusion | flops 1073741824 | bytes 9961472 | tf_op jit(solution)/shard_map/mrh,ph->mrp/dot_general | solution.py:31
  229.2 3.1 fusion.24
  232.3 0.7 reshape.46
  233.0 5.2 %all-to-all-start = ((f32[32,12,128]{2,1,0:T(8,128)}), f32[32,12,128]{2,1,0:T(8,128)S(1)}, u32[]{:S(2)}, u32[]{:S(2)}) async-start(f32[32,12,128]{2,1,0:T(8,128)} %reshape.46), calls=%async_computation | async-start | bytes 524288 | tf_op jit(solution)/shard_map/all_to_all | solution.py:81
  238.1 0.2 all-reduce.3.cloned.1.call-start
  238.4 4.7 %fusion.2 = f32[128,2048]{1,0:T(8,128)S(1)} fusion(bf16[1,2048,2048]{2,1,0:T(8,128)(2,1)} %all-gather.5.cloned.1.call-done, bf16[2,2048,128]{2,1,0:T(8,128)(2,1)S(1)} %copy-done.1), kind=kOutput, calls=%fused_computation.2 | convolution fusion | flops 1073741824 | bytes 9961472 | tf_op jit(solution)/shard_map/mrp,mrh->ph/dot_general | solution.py:33
  243.1 5.7 %fusion.18 = f32[128,2048]{1,0:T(8,128)} fusion(f32[128,2048]{1,0:T(8,128)S(1)} %fusion.2, bf16[1,2048,2048]{2,1,0:T(8,128)(2,1)} %all-gather.3.cloned.1.call-done, bf16[2,2048,128]{2,1,0:T(8,128)(2,1)S(1)} %copy-done.1), kind=kOutput, calls=%fused_computation.14 | convolution fusion | flops 1074003968 | bytes 11010048 | tf_op jit(solution)/shard_map/mrp,mrh->ph/dot_general | solution.py:33
  248.8 0.1 copy.23
  248.9 0.7 reshape.48
  249.6 0.1 constant_dynamic-slice_fusion.2
  249.7 0.1 copy.25
  249.8 0.1 copy.21
  250.0 120.6 %all-reduce.3.cloned.1.call-done = (f32[128,2048]{1,0:T(8,128)}, f32[4,12,1024]{2,0,1:T(4,128)}) async-done(((f32[128,2048]{1,0:T(8,128)}, f32[4,12,1024]{2,0,1:T(4,128)}), (f32[128,2048]{1,0:T(8,128)}, f32[4,12,1024]{2,0,1:T(4,128)})) %all-reduce.3.cloned.1.call-update) | async-done | bytes 1245200 | tf_op jit(solution)/shard_map/psum | solution.py:66
  370.6 2.1 fusion.33
  372.7 2.3 copy.30
  (23 shorter events, 0.2 us)
Async XLA Ops:
  7.2 112.3 %copy-start = (bf16[128,2048]{1,0:T(8,128)(2,1)S(1)}, bf16[128,2048]{1,0:T(8,128)(2,1)}, u32[]{:S(2)}) copy-start(bf16[128,2048]{1,0:T(8,128)(2,1)} %param.12) | copy-start | bytes 1572868
  7.2 112.3 %all-gather.5.cloned.1.call-start = ((), (), s32[]{:S(2)}) async-start(), calls=%async_computation.2 | async-start | bytes 8650752 | tf_op jit(solution)/shard_map/all_gather | solution.py:61
  9.2 214.1 %all-gather.3.cloned.1.call-start = ((), (), s32[]{:S(2)}) async-start(), calls=%async_computation.1 | async-start | bytes 8650752 | tf_op jit(solution)/shard_map/all_gather | solution.py:61
  126.2 103.0 %copy-start.6 = (bf16[2,2048,128]{2,1,0:T(8,128)(2,1)S(1)}, bf16[2,2048,128]{2,1,0:T(8,128)(2,1)}, u32[]{:S(2)}) copy-start(bf16[2,2048,128]{2,1,0:T(8,128)(2,1)} %param.10) | copy-start | bytes 3145732
  126.2 112.2 %copy-start.1 = (bf16[2,2048,128]{2,1,0:T(8,128)(2,1)S(1)}, bf16[2,2048,128]{2,1,0:T(8,128)(2,1)}, u32[]{:S(2)}) copy-start(bf16[2,2048,128]{2,1,0:T(8,128)(2,1)} %param.9) | copy-start | bytes 3145732
  223.3 5.9 %copy-start.7 = (f32[1,2048,128]{2,1,0:T(8,128)S(1)}, f32[1,2048,128]{2,1,0:T(8,128)}, u32[]{:S(2)}) copy-start(f32[1,2048,128]{2,1,0:T(8,128)} %fusion.15) | copy-start | bytes 3145732
  233.0 15.8 %all-to-all-start = ((f32[32,12,128]{2,1,0:T(8,128)}), f32[32,12,128]{2,1,0:T(8,128)S(1)}, u32[]{:S(2)}, u32[]{:S(2)}) async-start(f32[32,12,128]{2,1,0:T(8,128)} %reshape.46), calls=%async_computation | async-start | bytes 524288 | tf_op jit(solution)/shard_map/all_to_all | solution.py:81
  238.1 132.4 %all-reduce.3.cloned.1.call-start = ((), (), s32[]{:S(2)}) async-start(), calls=%async_computation.3 | async-start | bytes 2490368 | tf_op jit(solution)/shard_map/psum | solution.py:66
  243.0 6.6 %copy-start.5 = (s32[32,4,12]{0,1,2:T(4,128)S(1)}, s32[32,4,12]{0,1,2:T(4,128)}, u32[]{:S(2)}) copy-start(s32[32,4,12]{0,1,2:T(4,128)} %param.14) | copy-start | bytes 18436
  243.1 127.5 %copy-start.2 = (f32[1,4,12,1024]{3,1,2,0:T(4,128)S(1)}, f32[1,4,12,1024]{3,1,2,0:T(4,128)}, u32[]{:S(2)}) copy-start(f32[1,4,12,1024]{3,1,2,0:T(4,128)} %param.17) | copy-start | bytes 589828
  243.1 127.5 %copy-start.3 = (f32[1,4,12,1024]{3,1,2,0:T(4,128)S(1)}, f32[1,4,12,1024]{3,1,2,0:T(4,128)}, u32[]{:S(2)}) copy-start(f32[1,4,12,1024]{3,1,2,0:T(4,128)} %param.16) | copy-start | bytes 589828
  243.1 127.5 %copy-start.4 = (f32[1,4,12,1024]{3,1,2,0:T(4,128)S(1)}, f32[1,4,12,1024]{3,1,2,0:T(4,128)}, u32[]{:S(2)}) copy-start(f32[1,4,12,1024]{3,1,2,0:T(4,128)} %param.15) | copy-start | bytes 589828
Sparse Core Ops, SparseCore 0:
  11.7 107.6 all-gather.4
  122.6 100.5 all-gather.2
  249.8 120.7 all-reduce.2
where the time goes:
time: 382 us
  waiting for transfers between devices  326 us (85%)
  matrix products  26 us (7%)
  between operations  13.9 us (4%)
  local copies, waits for them, and re-layouts  7.9 us (2%)
  starting transfers between devices  5.46 us (1%)
    all_gather x2, waiting for transfers between devices, local(): lax.all_gather(query_grad[micro:micro + 1], 'table', axis=1, tiled=True)  205 us
    psum x1, waiting for transfers between devices, local(): weight_grad = lax.psum(wgrad, 'dp')  121 us
    dot_general x2, matrix products, make_step(): jnp.einsum('mrh,ph->mrp', piece, weight_part, preferred_element_type=jnp....  12.6 us
    dot_general x2, matrix products, make_step(): jnp.einsum('mrp,mrh->ph', emb_part, piece, preferred_element_type=jnp.flo...  10.4 us
  transfers between devices with their start and end apart: 4, of which 3 were waited for; matrix products, arithmetic and copies ran while one was open for 5% of the time, Pallas kernels for 0%

commit v1 on v0

--- a/solution.py
+++ b/solution.py
@@ -1,3 +1,4 @@
+import functools
 import jax
 import jax.numpy as jnp
 from jax import lax
@@ -10,6 +11,14 @@
 learn_rate = 0.01
 adam_eps = 1e-08
 adam_step = 10
+
+
+def quotas_build(x_part, axis_id):
+    block_out = jax.lax.all_gather(x_part, axis_id)
+    return jnp.sum(block_out, axis=0)
+
+
+bind_pipes = functools.partial(quotas_build, axis_id="dp")
 
 
 def adam_rows(grads, values, mean, square, live):
@@ -63,7 +72,7 @@
         backs.append(back_one)
     back_all = jnp.concatenate(backs, axis=0)
     emb_grad = resid_grad.astype(jnp.float32) + back_all
-    weight_grad = lax.psum(wgrad, "dp")
+    weight_grad = bind_pipes(wgrad)
     slice_idx = table_idx * width_part // SW
     ids = lax.dynamic_index_in_dim(ngram_rows, slice_idx, 2, False)
     listed = lax.dynamic_index_in_dim(touched_rows, slice_idx, 1, False)

time: 382 us -> 476 us (1.25)
  the two profiles are of different devices: /device:TPU:25 before, /device:TPU:1 now
where the time goes in v1:
time: 476 us
  waiting for transfers between devices  414 us (87%)
  matrix products  26 us (5%)
  between operations  13.9 us (3%)
  other arithmetic  10.6 us (2%)
  local copies, waits for them, and re-layouts  5.6 us (1%)
  starting transfers between devices  5.51 us (1%)
    all_gather x2, waiting for transfers between devices, local(): lax.all_gather(query_grad[micro:micro + 1], 'table', axis=1, tiled=True)  206 us
    psum x1, waiting for transfers between devices, local(): grads = lax.psum(local_grad, 'dp')  104 us
    all_gather x1, waiting for transfers between devices, quotas_build(): block_out = jax.lax.all_gather(x_part, axis_id)  98.7 us
    dot_general x2, matrix products, make_step(): jnp.einsum('mrh,ph->mrp', piece, weight_part, preferred_element_type=jnp....  12.6 us
    dot_general x2, matrix products, make_step(): jnp.einsum('mrp,mrh->ph', emb_part, piece, preferred_element_type=jnp.flo...  10.3 us
  transfers between devices with their start and end apart: 5, of which 5 were waited for; matrix products, arithmetic and copies ran while one was open for 4% of the time, Pallas kernels for 0%

profile of v1, /device:TPU:1, one launch (start us, length us, event | category | flops | bytes accessed | tf_op | source)
XLA Modules:
  0.0 475.8 jit_solution(15537818647815510272)
XLA Ops:
  7.2 1.9 fusion.37
  9.2 0.7 all-gather.5.cloned.1.call-update
  9.9 0.8 constant_dynamic-slice_fusion
  10.7 0.1 copy.22
  10.8 0.1 eq.19
  10.9 0.9 constant_dynamic-slice_fusion.1
  11.8 108.8 %all-gather.7.cloned.1.call-done = bf16[1,2048,2048]{2,1,0:T(8,128)(2,1)} async-done(((bf16[1,64,2048]{2,1,0:T(8,128)(2,1)}), bf16[1,2048,2048]{2,1,0:T(8,128)(2,1)}) %all-gather.7.cloned.1.call-update) | async-done | bytes 8388624 | tf_op jit(solution)/shard_map/all_gather | solution.py:70
  120.6 6.7 %fusion.15 = f32[1,2048,128]{2,1,0:T(8,128)} fusion(bf16[128,2048]{1,0:T(8,128)(2,1)S(1)} %copy-done, bf16[1,2048,2048]{2,1,0:T(8,128)(2,1)} %all-gather.7.cloned.1.call-done), kind=kOutput, calls=%fused_computation.13 | convolution fusion | flops 1073741824 | bytes 9961472 | tf_op jit(solution)/shard_map/mrh,ph->mrp/dot_general | solution.py:40
  127.3 97.1 %all-gather.5.cloned.1.call-done = bf16[1,2048,2048]{2,1,0:T(8,128)(2,1)} async-done(((bf16[1,64,2048]{2,1,0:T(8,128)(2,1)}), bf16[1,2048,2048]{2,1,0:T(8,128)(2,1)}) %all-gather.5.cloned.1.call-update) | async-done | bytes 8388624 | tf_op jit(solution)/shard_map/all_gather | solution.py:70
  224.4 5.8 %fusion.12 = f32[1,2048,128]{2,1,0:T(8,128)S(1)} fusion(bf16[128,2048]{1,0:T(8,128)(2,1)S(1)} %copy-done, bf16[1,2048,2048]{2,1,0:T(8,128)(2,1)} %all-gather.5.cloned.1.call-done), kind=kOutput, calls=%fused_computation.12 | convolution fusion | flops 1073741824 | bytes 9961472 | tf_op jit(solution)/shard_map/mrh,ph->mrp/dot_general | solution.py:40
  230.2 3.1 fusion.24
  233.3 0.7 reshape.46
  234.1 5.2 %all-to-all-start = ((f32[32,12,128]{2,1,0:T(8,128)}), f32[32,12,128]{2,1,0:T(8,128)S(1)}, u32[]{:S(2)}, u32[]{:S(2)}) async-start(f32[32,12,128]{2,1,0:T(8,128)} %reshape.46), calls=%async_computation | async-start | bytes 524288 | tf_op jit(solution)/shard_map/all_to_all | solution.py:90
  239.3 4.7 fusion.2
  244.0 4.9 %all-to-all-done = f32[32,12,128]{2,1,0:T(8,128)S(1)} async-done(((f32[32,12,128]{2,1,0:T(8,128)}), f32[32,12,128]{2,1,0:T(8,128)S(1)}, u32[]{:S(2)}, u32[]{:S(2)}) %all-to-all-start) | async-done | bytes 196640 | tf_op jit(solution)/shard_map/all_to_all | solution.py:90
  249.0 0.7 reshape.48
  249.8 0.2 all-gather.9.cloned.1.call-start
  250.0 5.7 %fusion.18 = f32[128,2048]{1,0:T(8,128)} fusion(f32[128,2048]{1,0:T(8,128)S(1)} %fusion.2, bf16[1,2048,2048]{2,1,0:T(8,128)(2,1)} %all-gather.5.cloned.1.call-done, bf16[2,2048,128]{2,1,0:T(8,128)(2,1)S(1)} %copy-done.1), kind=kOutput, calls=%fused_computation.14 | convolution fusion | flops 1074003968 | bytes 11010048 | tf_op jit(solution)/shard_map/mrp,mrh->ph/dot_general | solution.py:42
  255.8 0.1 copy.25
  255.9 0.1 copy.21
  256.0 104.0 %all-reduce.2.cloned.1.call-done = f32[4,12,1024]{2,0,1:T(4,128)} async-done(((f32[4,12,1024]{2,0,1:T(4,128)}), f32[4,12,1024]{2,0,1:T(4,128)}) %all-reduce.2.cloned.1.call-update) | async-done | bytes 196624 | tf_op jit(solution)/shard_map/psum | solution.py:102
  360.0 2.1 fusion.33
  362.2 98.7 %all-gather.9.cloned.1.call-done = f32[2048,2048]{1,0:T(8,128)} async-done(((f32[128,2048]{1,0:T(8,128)}), f32[2048,2048]{1,0:T(8,128)}) %all-gather.9.cloned.1.call-update) | async-done | bytes 16777232 | tf_op jit(solution)/shard_map/all_gather | solution.py:17
  460.8 8.4 %reduce_sum.9 = f32[128,2048]{1,0:T(8,128)} reduce(f32[16,128,2048]{2,1,0:T(8,128)} %bitcast.75, f32[]{:T(128)} %constant.22.clone.1), dimensions={0}, to_apply=%region_0.0 | reduce | flops 3932160 | bytes 17825796 | tf_op jit(solution)/shard_map/reduce_sum | solution.py:18
  (26 shorter events, 0.4 us)
Async XLA Ops:
  7.2 113.4 %copy-start = (bf16[128,2048]{1,0:T(8,128)(2,1)S(1)}, bf16[128,2048]{1,0:T(8,128)(2,1)}, u32[]{:S(2)}) copy-start(bf16[128,2048]{1,0:T(8,128)(2,1)} %param.12) | copy-start | bytes 1572868
  7.2 113.4 %all-gather.7.cloned.1.call-start = ((), (), s32[]{:S(2)}) async-start(), calls=%async_computation.2 | async-start | bytes 8650752 | tf_op jit(solution)/shard_map/all_gather | solution.py:70
  9.2 215.2 %all-gather.5.cloned.1.call-start = ((), (), s32[]{:S(2)}) async-start(), calls=%async_computation.1 | async-start | bytes 8650752 | tf_op jit(solution)/shard_map/all_gather | solution.py:70
  127.3 103.0 %copy-start.6 = (bf16[2,2048,128]{2,1,0:T(8,128)(2,1)S(1)}, bf16[2,2048,128]{2,1,0:T(8,128)(2,1)}, u32[]{:S(2)}) copy-start(bf16[2,2048,128]{2,1,0:T(8,128)(2,1)} %param.10) | copy-start | bytes 3145732
  127.3 112.0 %copy-start.1 = (bf16[2,2048,128]{2,1,0:T(8,128)(2,1)S(1)}, bf16[2,2048,128]{2,1,0:T(8,128)(2,1)}, u32[]{:S(2)}) copy-start(bf16[2,2048,128]{2,1,0:T(8,128)(2,1)} %param.9) | copy-start | bytes 3145732
  224.4 5.9 %copy-start.7 = (f32[1,2048,128]{2,1,0:T(8,128)S(1)}, f32[1,2048,128]{2,1,0:T(8,128)}, u32[]{:S(2)}) copy-start(f32[1,2048,128]{2,1,0:T(8,128)} %fusion.15) | copy-start | bytes 3145732
  234.1 14.8 %all-to-all-start = ((f32[32,12,128]{2,1,0:T(8,128)}), f32[32,12,128]{2,1,0:T(8,128)S(1)}, u32[]{:S(2)}, u32[]{:S(2)}) async-start(f32[32,12,128]{2,1,0:T(8,128)} %reshape.46), calls=%async_computation | async-start | bytes 524288 | tf_op jit(solution)/shard_map/all_to_all | solution.py:90
  239.2 120.8 %all-reduce.2.cloned.1.call-start = ((), (), s32[]{:S(2)}) async-start(), calls=%async_computation.3 | async-start | bytes 393216 | tf_op jit(solution)/shard_map/psum | solution.py:102
  249.7 6.0 %copy-start.5 = (s32[32,4,12]{0,1,2:T(4,128)S(1)}, s32[32,4,12]{0,1,2:T(4,128)}, u32[]{:S(2)}) copy-start(s32[32,4,12]{0,1,2:T(4,128)} %param.14) | copy-start | bytes 18436
  249.7 110.3 %copy-start.2 = (f32[1,4,12,1024]{3,1,2,0:T(4,128)S(1)}, f32[1,4,12,1024]{3,1,2,0:T(4,128)}, u32[]{:S(2)}) copy-start(f32[1,4,12,1024]{3,1,2,0:T(4,128)} %param.17) | copy-start | bytes 589828
  249.7 110.3 %copy-start.3 = (f32[1,4,12,1024]{3,1,2,0:T(4,128)S(1)}, f32[1,4,12,1024]{3,1,2,0:T(4,128)}, u32[]{:S(2)}) copy-start(f32[1,4,12,1024]{3,1,2,0:T(4,128)} %param.16) | copy-start | bytes 589828
  249.8 110.3 %copy-start.4 = (f32[1,4,12,1024]{3,1,2,0:T(4,128)S(1)}, f32[1,4,12,1024]{3,1,2,0:T(4,128)}, u32[]{:S(2)}) copy-start(f32[1,4,12,1024]{3,1,2,0:T(4,128)} %param.15) | copy-start | bytes 589828
  249.8 211.1 %all-gather.9.cloned.1.call-start = ((), (), s32[]{:S(2)}) async-start(), calls=%async_computation.4 | async-start | bytes 17825792 | tf_op jit(solution)/shard_map/all_gather | solution.py:17
Sparse Core Ops, SparseCore 0:
  11.7 108.7 all-gather.6
  123.7 100.5 all-gather.4
  249.8 110.1 all-reduce.1
  362.6 98.2 all-gather.8
